TPU v7x, 32 devices: a whole 2x2x4 slice. The times are simulated.
32 devices in a mesh: scene: 4 (over x, core), seq: 8 (over z, y).
Axes of the slice: x: 2, y: 2, z: 4, core: 2. Of those that a mesh axis runs over, the one named last changes fastest.
Arguments:
- tokens: bfloat16 [10240, 768], P(('scene', 'seq')), may hold values from -6 to 6
- scene_tokens: int32 [4], P('scene'), may hold values from 128 to 320, as said below
- cotangent: bfloat16 [10240, 768], P(('scene', 'seq')), may hold values from -6 to 6
- qkv_master: float32 [768, 2304], P(('scene', 'seq')), may hold values from -0.21875 to 0.21875
- out_master: float32 [768, 768], P(('scene', 'seq')), may hold values from -6 to 6
- up_master: float32 [768, 3072], P(('scene', 'seq')), may hold values from -0.21875 to 0.21875
- down_master: float32 [3072, 768], P(('scene', 'seq')), may hold values from -0.109375 to 0.109375
- gain_one: float32 [768], replicated, may hold values from 0.5 to 1.5
- gain_two: float32 [768], replicated, may hold values from 0.5 to 1.5
Outputs:
- mixed: bfloat16 [10240, 768], P(('scene', 'seq'))
- input_grad: float32 [10240, 768], P(('scene', 'seq'))
- qkv_grad: float32 [768, 2304], P(('scene', 'seq'))
- out_grad: float32 [768, 768], P(('scene', 'seq'))
- up_grad: float32 [768, 3072], P(('scene', 'seq'))
- down_grad: float32 [3072, 768], P(('scene', 'seq'))
- gain_one_grad: float32 [768], P(('scene', 'seq'))
- gain_two_grad: float32 [768], P(('scene', 'seq'))
Inputs may be any that keep to these rules, and one draw needn't show every extreme that they name: Slots 0 to scene_tokens[s] - 1 of every device of scene s's group hold that scene's tokens, the others are padding; one scene, drawn from the seed, has all 320 slots of every device live.
All inputs are finite; a program needn't handle non-finite values.
Results may differ from a plain program's by a relative error of at most 0.02.
Values may be sent and summed in bfloat16 or wider, within the bound.
No kernel may reach another device: no remote copies, remote signals or barrier semaphores. Data moves between devices by JAX's collectives and lax.ppermute only.
A program may use at most 512 MiB of HBM per device.

v0:
```python
import jax
import jax.numpy as jnp
from jax import lax
from jax.sharding import PartitionSpec as P

HEADS = 12
HEAD = 64
NEG_BIG = -1e30


def norm_rows(values, gain_vector):
    mean_value = jnp.mean(values, axis=-1, keepdims=True)
    centered = values - mean_value
    variance = jnp.mean(centered * centered, axis=-1, keepdims=True)
    inverse = lax.rsqrt(variance + 1e-05)
    scaled = centered * inverse
    return (scaled * gain_vector, scaled, inverse)


def norm_back(grad_result, scaled, inverse, gain_vector):
    grad_scaled = grad_result * gain_vector
    first_mean = jnp.mean(grad_scaled, axis=-1, keepdims=True)
    second_mean = jnp.mean(grad_scaled * scaled, axis=-1, keepdims=True)
    grad_input = inverse * (grad_scaled - first_mean - scaled * second_mean)
    return (grad_input, jnp.sum(grad_result * scaled, axis=0))


def split_heads(values):
    return values.reshape(values.shape[0], HEADS, HEAD)


def score_grads(query_part, grad_part, key_part, value_part, lse_part, delta_part, live_keys):
    scores = (
        jnp.einsum("qhd,khd->hqk", query_part, key_part, preferred_element_type=jnp.float32) * 0.125
    )
    weights_now = jnp.where(live_keys[None, None, :], jnp.exp(scores - lse_part[:, :, None]), 0.0)
    grad_weights = jnp.einsum(
        "qhd,khd->hqk", grad_part, value_part, preferred_element_type=jnp.float32
    )
    dscore = (weights_now * (grad_weights - delta_part[:, :, None])).astype(jnp.bfloat16)
    return (weights_now.astype(jnp.bfloat16), dscore)


def on_device(
    tokens,
    scene_tokens,
    cotangent,
    qkv_master,
    out_master,
    up_master,
    down_master,
    gain_one,
    gain_two,
):
    local_rows = tokens.shape[0]
    model_width = tokens.shape[1]
    live_count = scene_tokens[0]
    local_live = jnp.arange(local_rows, dtype=jnp.int32) < live_count
    qkv_part = qkv_master.astype(jnp.bfloat16)
    out_part = out_master.astype(jnp.bfloat16)
    up_part = up_master.astype(jnp.bfloat16)
    down_part = down_master.astype(jnp.bfloat16)
    qkv_weight, out_weight, up_weight, down_weight = (
        lax.all_gather(qkv_part, ("scene", "seq"), axis=0, tiled=True),
        lax.all_gather(out_part, ("scene", "seq"), axis=0, tiled=True),
        lax.all_gather(up_part, ("scene", "seq"), axis=0, tiled=True),
        lax.all_gather(down_part, ("scene", "seq"), axis=0, tiled=True),
    )
    inputs = tokens.astype(jnp.float32)
    normed_one, scaled_one, inverse_one = norm_rows(inputs, gain_one)
    normed_low = normed_one.astype(jnp.bfloat16)
    qkv_rows = jnp.dot(normed_low, qkv_weight, preferred_element_type=jnp.float32).astype(
        jnp.bfloat16
    )
    queries = qkv_rows[:, :model_width]
    key_rows = qkv_rows[:, model_width : 2 * model_width]
    value_rows = qkv_rows[:, 2 * model_width :]
    query_heads = split_heads(queries)

    def piece_live(piece_rows):
        places = jnp.arange(piece_rows, dtype=jnp.int32)
        return places % local_rows < live_count

    row_max = jnp.full((HEADS, local_rows), NEG_BIG, jnp.float32)
    key_piece = lax.all_gather(key_rows, "seq", axis=0, tiled=True)
    value_piece = lax.all_gather(value_rows, "seq", axis=0, tiled=True)
    piece_rows = key_piece.shape[0]
    scores = (
        jnp.einsum(
            "qhd,khd->hqk", query_heads, split_heads(key_piece), preferred_element_type=jnp.float32
        )
        * 0.125
    )
    scores = jnp.where(piece_live(piece_rows)[None, None, :], scores, NEG_BIG)
    new_max = jnp.maximum(row_max, jnp.max(scores, axis=-1))
    exponent = jnp.exp(scores - new_max[:, :, None])
    new_sum = jnp.sum(exponent, axis=-1)
    update = jnp.einsum(
        "hqk,khd->hqd",
        exponent.astype(jnp.bfloat16),
        split_heads(value_piece),
        preferred_element_type=jnp.float32,
    )
    row_lse = new_max + jnp.log(new_sum)
    attended = (
        (update / new_sum[:, :, None])
        .transpose(1, 0, 2)
        .reshape(local_rows, model_width)
        .astype(jnp.bfloat16)
    )
    resid = inputs + jnp.dot(attended, out_weight, preferred_element_type=jnp.float32)
    normed_two, scaled_two, inverse_two = norm_rows(resid, gain_two)
    normed_two_low = normed_two.astype(jnp.bfloat16)
    upper = jnp.dot(normed_two_low, up_weight, preferred_element_type=jnp.float32)
    activated, gelu_back = jax.vjp(jax.nn.gelu, upper)
    activated_low = activated.astype(jnp.bfloat16)
    mixed = (
        resid + jnp.dot(activated_low, down_weight, preferred_element_type=jnp.float32)
    ).astype(jnp.bfloat16)
    grad_result = cotangent.astype(jnp.float32) * local_live[:, None].astype(jnp.float32)
    grad_low = grad_result.astype(jnp.bfloat16)
    down_grad = jnp.einsum("tf,td->fd", activated_low, grad_low, preferred_element_type=jnp.float32)
    grad_active = jnp.einsum("td,fd->tf", grad_low, down_weight, preferred_element_type=jnp.float32)
    grad_upper = gelu_back(grad_active)[0].astype(jnp.bfloat16)
    up_grad = jnp.einsum(
        "td,tf->df", normed_two_low, grad_upper, preferred_element_type=jnp.float32
    )
    grad_normed_two = jnp.einsum(
        "tf,df->td", grad_upper, up_weight, preferred_element_type=jnp.float32
    )
    grad_norm_second, gain_two_grad = norm_back(grad_normed_two, scaled_two, inverse_two, gain_two)
    grad_resid = grad_result + grad_norm_second
    grad_branch = grad_resid.astype(jnp.bfloat16)
    out_grad = jnp.einsum("te,td->ed", attended, grad_branch, preferred_element_type=jnp.float32)
    grad_attended = jnp.einsum(
        "td,ed->te", grad_branch, out_weight, preferred_element_type=jnp.float32
    ).astype(jnp.bfloat16)
    grad_heads = split_heads(grad_attended)
    delta = jnp.sum(
        grad_heads.astype(jnp.float32) * split_heads(attended).astype(jnp.float32), axis=-1
    ).T
    total_rows = local_rows * lax.axis_size("seq")
    key_piece = lax.all_gather(key_rows, "seq", axis=0, tiled=True)
    value_piece = lax.all_gather(value_rows, "seq", axis=0, tiled=True)
    piece_rows = key_piece.shape[0]
    key_heads = split_heads(key_piece)
    weights_low, dscore = score_grads(
        query_heads,
        grad_heads,
        key_heads,
        split_heads(value_piece),
        row_lse,
        delta,
        piece_live(piece_rows),
    )
    grad_query = (
        jnp.einsum("hqk,khd->qhd", dscore, key_heads, preferred_element_type=jnp.float32) * 0.125
    )
    key_terms = (
        jnp.einsum("hqk,qhd->khd", dscore, query_heads, preferred_element_type=jnp.float32) * 0.125
    )
    value_terms = jnp.einsum(
        "hqk,qhd->khd", weights_low, grad_heads, preferred_element_type=jnp.float32
    )
    key_buffer = key_terms
    value_buffer = value_terms
    grad_query, key_buffer, value_buffer = (grad_query, key_buffer, value_buffer)
    grad_keys, grad_values = (
        lax.psum_scatter(
            key_buffer.reshape(total_rows, model_width).astype(jnp.bfloat16),
            "seq",
            scatter_dimension=0,
            tiled=True,
        ).astype(jnp.float32),
        lax.psum_scatter(
            value_buffer.reshape(total_rows, model_width).astype(jnp.bfloat16),
            "seq",
            scatter_dimension=0,
            tiled=True,
        ).astype(jnp.float32),
    )
    grad_qkv = jnp.concatenate(
        [grad_query.reshape(local_rows, model_width), grad_keys, grad_values], axis=1
    ).astype(jnp.bfloat16)
    qkv_grad = jnp.einsum("td,te->de", normed_low, grad_qkv, preferred_element_type=jnp.float32)
    grad_normed_one = jnp.einsum(
        "te,de->td", grad_qkv, qkv_weight, preferred_element_type=jnp.float32
    )
    grad_norm_first, gain_one_grad = norm_back(grad_normed_one, scaled_one, inverse_one, gain_one)
    input_grad = grad_resid + grad_norm_first
    qkv_share, out_share, up_share, down_share, first_share, second_share = (
        lax.psum_scatter(qkv_grad, ("scene", "seq"), scatter_dimension=0, tiled=True),
        lax.psum_scatter(out_grad, ("scene", "seq"), scatter_dimension=0, tiled=True),
        lax.psum_scatter(up_grad, ("scene", "seq"), scatter_dimension=0, tiled=True),
        lax.psum_scatter(down_grad, ("scene", "seq"), scatter_dimension=0, tiled=True),
        lax.psum_scatter(gain_one_grad, ("scene", "seq"), scatter_dimension=0, tiled=True),
        lax.psum_scatter(gain_two_grad, ("scene", "seq"), scatter_dimension=0, tiled=True),
    )
    return (
        mixed,
        input_grad,
        qkv_share,
        out_share,
        up_share,
        down_share,
        first_share,
        second_share,
    )


def solution(mesh):
    in_specs = (
        P(("scene", "seq"), None),
        P("scene"),
        P(("scene", "seq"), None),
        P(("scene", "seq"), None),
        P(("scene", "seq"), None),
        P(("scene", "seq"), None),
        P(("scene", "seq"), None),
        P(),
        P(),
    )
    out_specs = (
        P(("scene", "seq"), None),
        P(("scene", "seq"), None),
        P(("scene", "seq"), None),
        P(("scene", "seq"), None),
        P(("scene", "seq"), None),
        P(("scene", "seq"), None),
        P(("scene", "seq")),
        P(("scene", "seq")),
    )
    return jax.shard_map(
        on_device, mesh=mesh, in_specs=in_specs, out_specs=out_specs, check_vma=False
    )
```

profile of v0, /device:TPU:0, one launch (start us, length us, event | category | flops | bytes accessed | tf_op | source)
XLA Modules:
  0.0 1135.8 jit_solution(7848209360860348284)
XLA Ops:
  7.2 1.6 convert_element_type.98
  8.9 1.2 convert_reduce_fusion
  10.1 1.3 fusion.36
  11.4 63.0 %all-gather.7.cloned.1.call-done = bf16[768,2304]{1,0:T(8,128)(2,1)} async-done(((bf16[24,2304]{1,0:T(8,128)(2,1)}), bf16[768,2304]{1,0:T(8,128)(2,1)}) %all-gather.7.cloned.1.call-update) | async-done | bytes 3538960 | tf_op jit(solution)/shard_map/all_gather | solution.py:64
  74.4 3.6 convolution_convert_fusion
  78.0 1.0 fusion.66
  79.1 0.7 all-gather.11.cloned.1.call-update
  81.3 0.7 convert_element_type.107
  83.1 65.0 %all-gather.9.cloned.1.call-done = bf16[2560,768]{1,0:T(8,128)(2,1)} async-done(((bf16[320,768]{1,0:T(8,128)(2,1)}), bf16[2560,768]{1,0:T(8,128)(2,1)}) %all-gather.9.cloned.1.call-update) | async-done | bytes 3932176 | tf_op jit(solution)/shard_map/all_gather | solution.py:85
  148.1 6.3 copy.29
  154.4 17.1 %select_reduce_fusion = (f32[12,320]{1,0:T(8,128)S(1)}, f32[12,320,2560]{2,1,0:T(8,128)}) fusion(pred[2560]{0:T(1024)(128)(4,1)S(1)} %fusion.51, bf16[320,12,64]{0,2,1:T(8,128)(2,1)S(1)} %bitcast.50, bf16[2560,12,64]{0,2,1:T(8,128)(2,1)} %bitcast.47), kind=kOutput, calls=%fused_computation.3 | convolution fusion | flops 1287778560 | bytes 43763200 | tf_op jit(solution)/shard_map/qhd,khd->hqk/dot_general | solution.py:89
  171.5 47.9 %all-gather.11.cloned.1.call-done = bf16[2560,768]{1,0:T(8,128)(2,1)} async-done(((bf16[320,768]{1,0:T(8,128)(2,1)}), bf16[2560,768]{1,0:T(8,128)(2,1)}) %all-gather.11.cloned.1.call-update) | async-done | bytes 3932176 | tf_op jit(solution)/shard_map/all_gather | solution.py:86
  219.4 6.2 copy.30
  225.6 18.1 %fusion = f32[12,320]{1,0:T(8,128)S(1)} fusion(f32[12,320,2560]{2,1,0:T(8,128)} %get-tuple-element.20, f32[12,320]{1,0:T(8,128)S(1)} %broadcast_maximum_fusion, pred[2560]{0:T(1024)(128)(4,1)S(1)} %fusion.51), kind=kLoop, calls=%fused_computation.4 | loop fusion | flops 39317760 | bytes 39354880 | tf_op jit(solution)/shard_map/reduce_sum | solution.py:97
  243.8 15.2 %divide_convert_fusion = bf16[320,12,64]{0,2,1:T(8,128)(2,1)S(1)} fusion(bf16[2560,12,64]{0,2,1:T(8,128)(2,1)S(1)} %bitcast.55, f32[12,320,2560]{2,1,0:T(8,128)} %get-tuple-element.20, f32[12,320]{1,0:T(8,128)S(1)} %broadcast_maximum_fusion, pred[2560]{0:T(1024)(128)(4,1)S(1)} %fusion.51, f32[320,12]{0,1:T(8,128)S(1)} %bitcast.62), kind=kOutput, calls=%fused_computation.35 | convolution fusion | flops 1298104320 | bytes 43778560 | tf_op jit(solution)/shard_map/hqk,khd->hqd/dot_general | solution.py:98
  259.0 16.4 %all-gather.13.cloned.1.call-done = bf16[768,768]{1,0:T(8,128)(2,1)} async-done(((bf16[24,768]{1,0:T(8,128)(2,1)}), bf16[768,768]{1,0:T(8,128)(2,1)}) %all-gather.13.cloned.1.call-update) | async-done | bytes 1179664 | tf_op jit(solution)/shard_map/all_gather | solution.py:65
  275.4 1.9 fusion.67
  278.2 63.0 %all-gather.15.cloned.1.call-done = bf16[768,3072]{1,0:T(8,128)(2,1)} async-done(((bf16[24,3072]{1,0:T(8,128)(2,1)}), bf16[768,3072]{1,0:T(8,128)(2,1)}) %all-gather.15.cloned.1.call-update) | async-done | bytes 4718608 | tf_op jit(solution)/shard_map/all_gather | solution.py:66
  341.3 6.0 fusion.65
  347.3 59.8 %all-gather.17.cloned.1.call-done = bf16[3072,768]{1,0:T(8,128)(2,1)} async-done(((bf16[96,768]{1,0:T(8,128)(2,1)}), bf16[3072,768]{1,0:T(8,128)(2,1)}) %all-gather.17.cloned.1.call-update) | async-done | bytes 4718608 | tf_op jit(solution)/shard_map/all_gather | solution.py:67
  407.1 7.8 fusion.18
  415.0 2.5 multiply_reduce_fusion.1
  418.5 1.1 copy.31
  419.5 18.2 %fusion.9 = bf16[12,64,2560]{2,1,0:T(8,128)(2,1)} fusion(bf16[320,12,64]{0,2,1:T(8,128)(2,1)} %bitcast.59, f32[12,320,2560]{2,1,0:T(8,128)} %get-tuple-element.20, f32[12,320]{1,0:T(8,128)} %log_add_fusion, pred[2560]{0:T(1024)(128)(4,1)S(1)} %fusion.51), kind=kOutput, calls=%fused_computation.14 | convolution fusion | flops 1299578880 | bytes 43763200 | tf_op jit(solution)/shard_map/hqk,qhd->khd/dot_general | solution.py:162
  437.7 6.3 copy.34
  444.1 1.4 multiply_reduce_fusion
  445.6 26.5 %multiply_convert_fusion = bf16[12,320,2560]{2,1,0:T(8,128)(2,1)} fusion(f32[12,320,2560]{2,1,0:T(8,128)} %get-tuple-element.20, bf16[320,12,64]{0,2,1:T(8,128)(2,1)} %bitcast.61, bf16[2560,12,64]{0,2,1:T(8,128)(2,1)} %bitcast.54, f32[12,320]{1,0:T(8,128)S(1)} %bitcast.63, f32[12,320]{1,0:T(8,128)S(1)} %copy-done.19, pred[2560]{0:T(1024)(128)(4,1)S(1)} %fusion.51), kind=kOutput, calls=%fused_computation | convolution fusion | flops 1317273600 | bytes 63439360 | tf_op jit(solution)/shard_map/qhd,khd->hqk/dot_general | solution.py:37
  472.1 12.6 %multiply_convert_fusion.1 = bf16[12,64,2560]{2,1,0:T(8,128)(2,1)} fusion(bf16[320,12,64]{0,2,1:T(8,128)(2,1)S(1)} %bitcast.51, bf16[12,320,2560]{2,1,0:T(8,128)(2,1)} %multiply_convert_fusion), kind=kOutput, calls=%fused_computation.11 | convolution fusion | flops 1262223360 | bytes 24084480 | tf_op jit(solution)/shard_map/hqk,qhd->khd/dot_general | solution.py:160
  484.7 6.3 copy.32
  491.1 1.0 copy-done.2
  492.1 2.2 fusion.42
  494.3 6.8 fusion.64
  501.2 1.0 copy-done.9
  502.2 8.7 fusion.45
  511.0 10.9 fusion.23
  522.0 5.4 reduce-scatter.21.cloned.1.call-done
  527.4 2.1 copy.35
  529.5 86.1 %reduce-scatter.19.cloned.1.call-done = bf16[320,768]{1,0:T(8,128)(2,1)} async-done(((bf16[2560,768]{1,0:T(8,128)(2,1)}), bf16[320,768]{1,0:T(8,128)(2,1)}) %reduce-scatter.19.cloned.1.call-update) | async-done | bytes 491536
  615.6 2.1 copy.33
  617.7 6.4 fusion.38
  624.1 6.9 fusion.22
  631.0 1.9 fusion.35
  632.9 40.4 %all-reduce.2 = (f32[768]{0:T(1024)S(1)}, f32[768]{0:T(1024)S(1)}) all-reduce(f32[768]{0:T(1024)S(1)} %get-tuple-element.10, f32[768]{0:T(1024)S(1)} %copy-done.23), channel_id=8, replica_groups=mesh['scene'=4,'seq'=8] {'scene','seq'}, use_global_device_ids=true, to_apply=%region_18.19.clone | all-reduce | flops 1536 | bytes 12288
  674.5 1.3 fusion.34
  675.8 44.5 %reduce-scatter.13.cloned.1.call-done = f32[24,768]{1,0:T(8,128)} async-done(((f32[768,768]{1,0:T(8,128)}), f32[24,768]{1,0:T(8,128)}) %reduce-scatter.13.cloned.1.call-update) | async-done | bytes 73744 | tf_op jit(solution)/shard_map/reduce_scatter | solution.py:193
  720.3 142.0 %reduce-scatter.15.cloned.1.call-done = f32[24,3072]{1,0:T(8,128)} async-done(((f32[768,3072]{1,0:T(8,128)}), f32[24,3072]{1,0:T(8,128)}) %reduce-scatter.15.cloned.1.call-update) | async-done | bytes 294928 | tf_op jit(solution)/shard_map/reduce_scatter | solution.py:194
  862.3 141.0 %reduce-scatter.17.cloned.1.call-done = f32[96,768]{1,0:T(8,128)} async-done(((f32[3072,768]{1,0:T(8,128)}), f32[96,768]{1,0:T(8,128)}) %reduce-scatter.17.cloned.1.call-update) | async-done | bytes 294928 | tf_op jit(solution)/shard_map/reduce_scatter | solution.py:195
  1003.3 125.4 %reduce-scatter.11.cloned.1.call-done = f32[24,2304]{1,0:T(8,128)} async-done(((f32[768,2304]{1,0:T(8,128)}), f32[24,2304]{1,0:T(8,128)}) %reduce-scatter.11.cloned.1.call-update) | async-done | bytes 221200 | tf_op jit(solution)/shard_map/reduce_scatter | solution.py:192
  (92 shorter events, 5.5 us)
Async XLA Ops:
  7.2 67.2 %all-gather.7.cloned.1.call-start = ((), (), s32[]{:S(2)}) async-start(), calls=%async_computation.6 | async-start | bytes 3649536 | tf_op jit(solution)/shard_map/all_gather | solution.py:64
  8.8 139.3 %all-gather.9.cloned.1.call-start = ((), (), s32[]{:S(2)}) async-start(), calls=%async_computation.7 | async-start | bytes 4423680 | tf_op jit(solution)/shard_map/all_gather | solution.py:85
  10.1 64.3 %copy-start.15 = (f32[320]{0:T(512)}, f32[320]{0:T(512)S(1)}, u32[]{:S(2)}) copy-start(f32[320]{0:T(512)S(1)} %broadcast_multiply_fusion.5) | copy-start | bytes 3844
  11.4 63.0 %copy-start.17 = (f32[320]{0:T(512)}, f32[320]{0:T(512)S(1)}, u32[]{:S(2)}) copy-start(f32[320]{0:T(512)S(1)} %add_rsqrt_fusion.1) | copy-start | bytes 3844
  78.0 1.9 copy-start.14
  78.0 2.6 copy-start.10
  78.0 3.3 copy-start.11
  79.1 140.3 %all-gather.11.cloned.1.call-start = ((), (), s32[]{:S(2)}) async-start(), calls=%async_computation.8 | async-start | bytes 4423680 | tf_op jit(solution)/shard_map/all_gather | solution.py:86
  79.8 195.6 %all-gather.13.cloned.1.call-start = ((), (), s32[]{:S(2)}) async-start(), calls=%async_computation.9 | async-start | bytes 1216512 | tf_op jit(solution)/shard_map/all_gather | solution.py:65
  80.5 260.8 %all-gather.15.cloned.1.call-start = ((), (), s32[]{:S(2)}) async-start(), calls=%async_computation.10 | async-start | bytes 4866048 | tf_op jit(solution)/shard_map/all_gather | solution.py:66
  81.3 325.8 %all-gather.17.cloned.1.call-start = ((), (), s32[]{:S(2)}) async-start(), calls=%async_computation.11 | async-start | bytes 4866048 | tf_op jit(solution)/shard_map/all_gather | solution.py:67
  82.0 445.4 %reduce-scatter.21.cloned.1.call-start = ((), (), s32[]{:S(2)}) async-start(), calls=%async_computation.17 | async-start | bytes 4423680
  82.8 324.4 %copy-start.20 = (f32[320]{0:T(512)}, f32[320]{0:T(512)S(1)}, u32[]{:S(2)}) copy-start(f32[320]{0:T(512)S(1)} %fusion.55) | copy-start | bytes 3844
  225.6 18.1 %copy-start.4 = (bf16[2560,768]{0,1:T(8,128)(2,1)S(1)}, bf16[2560,768]{0,1:T(8,128)(2,1)}, u32[]{:S(2)}) copy-start(bf16[2560,768]{0,1:T(8,128)(2,1)} %copy.30) | copy-start | bytes 11796484
  243.7 31.6 %copy-start = (bf16[320,768]{1,0:T(8,128)(2,1)S(1)}, bf16[320,768]{1,0:T(8,128)(2,1)}, u32[]{:S(2)}) copy-start(bf16[320,768]{1,0:T(8,128)(2,1)} %param.9) | copy-start | bytes 1474564
  259.0 88.3 %copy-start.1 = (bf16[320,12,64]{0,2,1:T(8,128)(2,1)}, bf16[320,12,64]{0,2,1:T(8,128)(2,1)S(1)}, u32[]{:S(2)}) copy-start(bf16[320,12,64]{0,2,1:T(8,128)(2,1)S(1)} %divide_convert_fusion) | copy-start | bytes 1474564
  259.0 82.3 %copy-start.12 = (f32[768]{0:T(1024)S(1)}, f32[768]{0:T(1024)}, u32[]{:S(2)}) copy-start(f32[768]{0:T(1024)} %param.17) | copy-start | bytes 9220
  278.2 128.9 %copy-start.8 = (bf16[320,768]{1,0:T(8,128)(2,1)S(1)}, bf16[320,768]{1,0:T(8,128)(2,1)}, u32[]{:S(2)}) copy-start(bf16[320,768]{1,0:T(8,128)(2,1)} %param.11) | copy-start | bytes 1474564
  407.1 7.8 copy-start.24
  415.0 2.5 copy-start.7
  415.0 2.5 copy-start.21
  415.0 2.9 copy-start.3
  444.1 1.5 copy-start.19
  444.1 171.5 %reduce-scatter.19.cloned.1.call-start = ((), (), s32[]{:S(2)}) async-start(), calls=%async_computation.16 | async-start | bytes 4423680
  491.0 1.1 copy-start.2
  491.0 229.3 %reduce-scatter.13.cloned.1.call-start = ((), (), s32[]{:S(2)}) async-start(), calls=%async_computation.13 | async-start | bytes 2433024 | tf_op jit(solution)/shard_map/reduce_scatter | solution.py:193
  494.3 368.1 %reduce-scatter.15.cloned.1.call-start = ((), (), s32[]{:S(2)}) async-start(), calls=%async_computation.14 | async-start | bytes 9732096 | tf_op jit(solution)/shard_map/reduce_scatter | solution.py:194
  501.2 1.0 copy-start.9
  501.2 1.0 copy-start.22
  501.2 502.1 %reduce-scatter.17.cloned.1.call-start = ((), (), s32[]{:S(2)}) async-start(), calls=%async_computation.15 | async-start | bytes 9732096 | tf_op jit(solution)/shard_map/reduce_scatter | solution.py:195
  511.0 106.7 %copy-start.13 = (f32[768]{0:T(1024)S(1)}, f32[768]{0:T(1024)}, u32[]{:S(2)}) copy-start(f32[768]{0:T(1024)} %param.16) | copy-start | bytes 9220
  511.0 106.7 %copy-start.16 = (f32[320]{0:T(512)S(1)}, f32[320]{0:T(512)}, u32[]{:S(2)}) copy-start(f32[320]{0:T(512)} %copy-done.15) | copy-start | bytes 3844
  511.0 106.7 %copy-start.18 = (f32[320]{0:T(512)S(1)}, f32[320]{0:T(512)}, u32[]{:S(2)}) copy-start(f32[320]{0:T(512)} %copy-done.17) | copy-start | bytes 3844
  511.0 617.7 %reduce-scatter.11.cloned.1.call-start = ((), (), s32[]{:S(2)}) async-start(), calls=%async_computation.12 | async-start | bytes 7299072 | tf_op jit(solution)/shard_map/reduce_scatter | solution.py:192
  624.1 6.9 copy-start.5
  624.1 6.9 copy-start.6
  624.1 6.9 copy-start.25
  631.0 1.9 copy-start.23
Sparse Core Ops, SparseCore 0:
  11.5 62.8 all-gather.6
  79.2 68.8 all-gather.8
  150.9 68.4 all-gather.10
  222.7 52.6 all-gather.12
  278.7 62.5 all-gather.14
  344.6 62.4 all-gather.16
  444.2 83.1 reduce-scatter.20
  531.5 83.9 reduce-scatter.18
  621.4 98.8 reduce-scatter.12
  727.6 134.6 reduce-scatter.14
  868.8 134.4 reduce-scatter.16
  1010.4 118.2 reduce-scatter.10
where the time goes:
time: 1150 us; the launch traced here: 1140 us
  waiting for transfers between devices  860 us (75%)
  matrix products  156 us (14%)
  blocking collectives  40.4 us (4%)
  local copies, waits for them, and re-layouts  35 us (3%)
  other arithmetic  28.3 us (2%)
  between operations  15.4 us (1%)
    reduce_scatter x1, waiting for transfers between devices, on_device(): lax.psum_scatter(up_grad, ('scene', 'seq'), scatter_dimension=0, tiled=True)  142 us
    reduce_scatter x1, waiting for transfers between devices, on_device(): lax.psum_scatter(down_grad, ('scene', 'seq'), scatter_dimension=0, tiled=...  141 us
    reduce_scatter x1, waiting for transfers between devices, on_device(): lax.psum_scatter(qkv_grad, ('scene', 'seq'), scatter_dimension=0, tiled=T...  125 us
    unnamed x14, waiting for transfers between devices  92.4 us
    all_gather x1, waiting for transfers between devices, on_device(): key_piece = lax.all_gather(key_rows, 'seq', axis=0, tiled=True)  65 us
    all_gather x1, waiting for transfers between devices, on_device(): lax.all_gather(up_part, ('scene', 'seq'), axis=0, tiled=True)  63 us
    all_gather x1, waiting for transfers between devices, on_device(): lax.all_gather(qkv_part, ('scene', 'seq'), axis=0, tiled=True)  63 us
    all_gather x1, waiting for transfers between devices, on_device(): lax.all_gather(down_part, ('scene', 'seq'), axis=0, tiled=True)  59.8 us
  transfers between devices with their start and end apart: 12, of which 12 were waited for; matrix products, arithmetic and copies ran while one was open for 15% of the time, Pallas kernels for 0%

commit v1 on v0

--- a/solution.py
+++ b/solution.py
@@ -82,8 +82,11 @@
         return places % local_rows < live_count
 
     row_max = jnp.full((HEADS, local_rows), NEG_BIG, jnp.float32)
-    key_piece = lax.all_gather(key_rows, "seq", axis=0, tiled=True)
-    value_piece = lax.all_gather(value_rows, "seq", axis=0, tiled=True)
+    key_piece, value_piece = jnp.split(
+        lax.all_gather(jnp.concatenate([key_rows, value_rows], axis=1), "seq", axis=0, tiled=True),
+        [key_rows.shape[1]],
+        axis=1,
+    )
     piece_rows = key_piece.shape[0]
     scores = (
         jnp.einsum(

time: 1150 us -> 1280 us (1.11)
  waiting for transfers between devices: 860 us -> 965 us
  local copies, waits for them, and re-layouts: 35 us -> 53.8 us
  matrix products: 156 us -> 173 us
    all_gather x0 -> x1, waiting for transfers between devices: none -> 113 us  [on_device(): lax.all_gather(jnp.concatenate([key_rows, value_rows], axis=1), 'seq', ax...]
    unnamed x14 -> x15, waiting for transfers between devices: 92.4 us -> 114 us
    split x0 -> x3, local copies, waits for them, and re-layouts: none -> 17.9 us  [on_device(): jnp.split(lax.all_gather(jnp.concatenate([key_rows, value_rows], axis=1),...]
    dot_general x0 -> x1, matrix products: none -> 17 us  [score_grads(): jnp.einsum('qhd,khd->hqk', query_part, key_part, preferred_element_type=j...]
    all_gather x1, waiting for transfers between devices: 16.4 us -> 0.02 us  [on_device(): lax.all_gather(out_part, ('scene', 'seq'), axis=0, tiled=True)]
    all_gather x1, waiting for transfers between devices: 63 us -> 49.8 us  [on_device(): lax.all_gather(up_part, ('scene', 'seq'), axis=0, tiled=True)]
  transfers between devices with their start and end apart: 12 -> 13, of which waited for: 12 -> 12; matrix products, arithmetic and copies ran while one was open for 15% -> 15% of each run, Pallas kernels for 0% -> 0%
where the time goes in v1:
time: 1280 us
  waiting for transfers between devices  965 us (75%)
  matrix products  173 us (14%)
  local copies, waits for them, and re-layouts  53.8 us (4%)
  blocking collectives  40.4 us (3%)
  other arithmetic  28.3 us (2%)
  between operations  15.2 us (1%)
    reduce_scatter x1, waiting for transfers between devices, on_device(): lax.psum_scatter(down_grad, ('scene', 'seq'), scatter_dimension=0, tiled=...  142 us
    reduce_scatter x1, waiting for transfers between devices, on_device(): lax.psum_scatter(up_grad, ('scene', 'seq'), scatter_dimension=0, tiled=True)  141 us
    reduce_scatter x1, waiting for transfers between devices, on_device(): lax.psum_scatter(qkv_grad, ('scene', 'seq'), scatter_dimension=0, tiled=T...  125 us
    unnamed x15, waiting for transfers between devices  114 us
    all_gather x1, waiting for transfers between devices, on_device(): lax.all_gather(jnp.concatenate([key_rows, value_rows], axis=1), 'seq', ax...  113 us
    all_gather x1, waiting for transfers between devices, on_device(): key_piece = lax.all_gather(key_rows, 'seq', axis=0, tiled=True)  63.6 us
    all_gather x1, waiting for transfers between devices, on_device(): lax.all_gather(qkv_part, ('scene', 'seq'), axis=0, tiled=True)  63 us
    all_gather x1, waiting for transfers between devices, on_device(): lax.all_gather(down_part, ('scene', 'seq'), axis=0, tiled=True)  60 us
  transfers between devices with their start and end apart: 13, of which 12 were waited for; matrix products, arithmetic and copies ran while one was open for 15% of the time, Pallas kernels for 0%

profile of v1, /device:TPU:0, one launch (start us, length us, event | category | flops | bytes accessed | tf_op | source)
XLA Modules:
  0.0 1275.6 jit_solution(11758598934167377349)
XLA Ops:
  7.2 1.6 convert_element_type.98
  8.9 1.2 convert_reduce_fusion
  10.1 1.3 fusion.37
  11.4 63.0 %all-gather.8.cloned.1.call-done = bf16[768,2304]{1,0:T(8,128)(2,1)} async-done(((bf16[24,2304]{1,0:T(8,128)(2,1)}), bf16[768,2304]{1,0:T(8,128)(2,1)}) %all-gather.8.cloned.1.call-update) | async-done | bytes 3538960 | tf_op jit(solution)/shard_map/all_gather | solution.py:64
  74.4 3.6 convolution_convert_fusion
  78.0 1.1 fusion.68
  84.5 63.6 %all-gather.18.cloned.1.call-done = bf16[2560,768]{1,0:T(8,128)(2,1)} async-done(((bf16[320,768]{1,0:T(8,128)(2,1)}), bf16[2560,768]{1,0:T(8,128)(2,1)}) %all-gather.18.cloned.1.call-update) | async-done | bytes 3932176 | tf_op jit(solution)/shard_map/all_gather | solution.py:146
  148.1 6.3 copy.35
  154.4 17.0 %fusion.70 = f32[12,320,2560]{2,1,0:T(8,128)} fusion(bf16[320,12,64]{0,2,1:T(8,128)(2,1)S(1)} %bitcast.55, bf16[2560,12,64]{0,2,1:T(8,128)(2,1)} %bitcast.51), kind=kOutput, calls=%fused_computation.96 | convolution fusion | flops 1258291200 | bytes 43745280 | tf_op jit(solution)/shard_map/qhd,khd->hqk/dot_general | solution.py:34
  171.4 48.0 %all-gather.20.cloned.1.call-done = bf16[2560,768]{1,0:T(8,128)(2,1)} async-done(((bf16[320,768]{1,0:T(8,128)(2,1)}), bf16[2560,768]{1,0:T(8,128)(2,1)}) %all-gather.20.cloned.1.call-update) | async-done | bytes 3932176 | tf_op jit(solution)/shard_map/all_gather | solution.py:147
  219.4 6.2 copy.37
  225.6 113.2 %all-gather.10.cloned.1.call-done = bf16[2560,1536]{1,0:T(8,128)(2,1)} async-done(((bf16[320,1536]{1,0:T(8,128)(2,1)}), bf16[2560,1536]{1,0:T(8,128)(2,1)}) %all-gather.10.cloned.1.call-update) | async-done | bytes 7864336 | tf_op jit(solution)/shard_map/all_gather | solution.py:86
  338.8 5.5 fusion.67
  344.3 6.2 copy.33
  350.5 17.0 %fusion = (f32[12,320]{1,0:T(8,128)S(1)}, f32[12,320,2560]{2,1,0:T(8,128)}) fusion(pred[2560]{0:T(1024)(128)(4,1)S(1)} %fusion.52, bf16[320,12,64]{0,2,1:T(8,128)(2,1)S(1)} %bitcast.56, bf16[2560,12,64]{0,2,1:T(8,128)(2,1)} %bitcast.53), kind=kOutput, calls=%fused_computation.4 | convolution fusion | flops 1287778560 | bytes 43763200 | tf_op jit(solution)/shard_map/qhd,khd->hqk/dot_general | solution.py:92
  367.5 6.2 copy.34
  373.7 18.1 %fusion.1 = f32[12,320]{1,0:T(8,128)S(1)} fusion(f32[12,320,2560]{2,1,0:T(8,128)} %get-tuple-element.22, f32[12,320]{1,0:T(8,128)S(1)} %broadcast_maximum_fusion, pred[2560]{0:T(1024)(128)(4,1)S(1)} %fusion.52), kind=kLoop, calls=%fused_computation.5 | loop fusion | flops 39317760 | bytes 39354880 | tf_op jit(solution)/shard_map/reduce_sum | solution.py:100
  391.8 15.7 %divide_convert_fusion = bf16[320,12,64]{0,2,1:T(8,128)(2,1)S(1)} fusion(bf16[2560,12,64]{0,2,1:T(8,128)(2,1)S(1)} %bitcast.61, f32[12,320,2560]{2,1,0:T(8,128)} %get-tuple-element.22, f32[12,320]{1,0:T(8,128)S(1)} %broadcast_maximum_fusion, pred[2560]{0:T(1024)(128)(4,1)S(1)} %fusion.52, f32[320,12]{0,1:T(8,128)S(1)} %bitcast.68), kind=kOutput, calls=%fused_computation.36 | convolution fusion | flops 1298104320 | bytes 43778560 | tf_op jit(solution)/shard_map/hqk,khd->hqd/dot_general | solution.py:101
  407.7 2.1 fusion.69
  410.7 49.8 %all-gather.14.cloned.1.call-done = bf16[768,3072]{1,0:T(8,128)(2,1)} async-done(((bf16[24,3072]{1,0:T(8,128)(2,1)}), bf16[768,3072]{1,0:T(8,128)(2,1)}) %all-gather.14.cloned.1.call-update) | async-done | bytes 4718608 | tf_op jit(solution)/shard_map/all_gather | solution.py:66
  460.5 6.0 fusion.66
  466.4 60.0 %all-gather.16.cloned.1.call-done = bf16[3072,768]{1,0:T(8,128)(2,1)} async-done(((bf16[96,768]{1,0:T(8,128)(2,1)}), bf16[3072,768]{1,0:T(8,128)(2,1)}) %all-gather.16.cloned.1.call-update) | async-done | bytes 4718608 | tf_op jit(solution)/shard_map/all_gather | solution.py:67
  526.5 7.4 fusion.19
  533.9 2.5 multiply_reduce_fusion.1
  537.4 1.1 copy.36
  538.4 1.4 multiply_reduce_fusion
  539.9 26.1 %multiply_convert_fusion = bf16[12,320,2560]{2,1,0:T(8,128)(2,1)} fusion(f32[12,320,2560]{2,1,0:T(8,128)} %fusion.70, bf16[320,12,64]{0,2,1:T(8,128)(2,1)} %bitcast.66, bf16[2560,12,64]{0,2,1:T(8,128)(2,1)} %bitcast.60, f32[12,320]{1,0:T(8,128)S(1)} %bitcast.69, f32[12,320]{1,0:T(8,128)} %log_add_fusion, pred[2560]{0:T(1024)(128)(4,1)S(1)} %fusion.52), kind=kOutput, calls=%fused_computation | convolution fusion | flops 1317273600 | bytes 63439360 | tf_op jit(solution)/shard_map/qhd,khd->hqk/dot_general | solution.py:37
  565.9 12.4 multiply_convert_fusion.1
  578.3 6.2 copy.38
  585.6 18.3 %fusion.10 = bf16[12,64,2560]{2,1,0:T(8,128)(2,1)} fusion(bf16[320,12,64]{0,2,1:T(8,128)(2,1)S(1)} %bitcast.67, f32[12,320,2560]{2,1,0:T(8,128)} %fusion.70, f32[12,320]{1,0:T(8,128)S(1)} %copy-done.20, pred[2560]{0:T(1024)(128)(4,1)S(1)} %fusion.52), kind=kOutput, calls=%fused_computation.15 | convolution fusion | flops 1299578880 | bytes 43763200 | tf_op jit(solution)/shard_map/hqk,qhd->khd/dot_general | solution.py:165
  603.9 6.3 copy.40
  611.3 2.2 fusion.43
  613.6 8.7 fusion.46
  622.4 6.9 fusion.65
  629.4 11.1 fusion.24
  640.4 27.4 %reduce-scatter.19.cloned.1.call-done = bf16[320,768]{1,0:T(8,128)(2,1)} async-done(((bf16[2560,768]{1,0:T(8,128)(2,1)}), bf16[320,768]{1,0:T(8,128)(2,1)}) %reduce-scatter.19.cloned.1.call-update) | async-done | bytes 491536
  667.9 2.1 copy.39
  669.9 86.1 %reduce-scatter.21.cloned.1.call-done = bf16[320,768]{1,0:T(8,128)(2,1)} async-done(((bf16[2560,768]{1,0:T(8,128)(2,1)}), bf16[320,768]{1,0:T(8,128)(2,1)}) %reduce-scatter.21.cloned.1.call-update) | async-done | bytes 491536
  756.1 2.1 copy.41
  758.1 6.4 fusion.39
  764.6 6.9 fusion.23
  771.5 1.9 fusion.36
  773.4 40.4 %all-reduce.2 = (f32[768]{0:T(1024)S(1)}, f32[768]{0:T(1024)S(1)}) all-reduce(f32[768]{0:T(1024)S(1)} %get-tuple-element.10, f32[768]{0:T(1024)S(1)} %copy-done.24), channel_id=8, replica_groups=mesh['scene'=4,'seq'=8] {'scene','seq'}, use_global_device_ids=true, to_apply=%region_18.19.clone | all-reduce | flops 1536 | bytes 12288
  815.0 1.3 fusion.35
  816.3 44.3 %reduce-scatter.13.cloned.1.call-done = f32[24,768]{1,0:T(8,128)} async-done(((f32[768,768]{1,0:T(8,128)}), f32[24,768]{1,0:T(8,128)}) %reduce-scatter.13.cloned.1.call-update) | async-done | bytes 73744 | tf_op jit(solution)/shard_map/reduce_scatter | solution.py:196
  860.6 142.0 %reduce-scatter.17.cloned.1.call-done = f32[96,768]{1,0:T(8,128)} async-done(((f32[3072,768]{1,0:T(8,128)}), f32[96,768]{1,0:T(8,128)}) %reduce-scatter.17.cloned.1.call-update) | async-done | bytes 294928 | tf_op jit(solution)/shard_map/reduce_scatter | solution.py:198
  1002.7 140.9 %reduce-scatter.15.cloned.1.call-done = f32[24,3072]{1,0:T(8,128)} async-done(((f32[768,3072]{1,0:T(8,128)}), f32[24,3072]{1,0:T(8,128)}) %reduce-scatter.15.cloned.1.call-update) | async-done | bytes 294928 | tf_op jit(solution)/shard_map/reduce_scatter | solution.py:197
  1143.6 125.2 %reduce-scatter.11.cloned.1.call-done = f32[24,2304]{1,0:T(8,128)} async-done(((f32[768,2304]{1,0:T(8,128)}), f32[24,2304]{1,0:T(8,128)}) %reduce-scatter.11.cloned.1.call-update) | async-done | bytes 221200 | tf_op jit(solution)/shard_map/reduce_scatter | solution.py:195
  (102 shorter events, 10.2 us)
Async XLA Ops:
  7.2 67.2 %all-gather.8.cloned.1.call-start = ((), (), s32[]{:S(2)}) async-start(), calls=%async_computation.6 | async-start | bytes 3649536 | tf_op jit(solution)/shard_map/all_gather | solution.py:64
  8.8 139.3 %all-gather.18.cloned.1.call-start = ((), (), s32[]{:S(2)}) async-start(), calls=%async_computation.11 | async-start | bytes 4423680 | tf_op jit(solution)/shard_map/all_gather | solution.py:146
  10.1 64.3 %copy-start.16 = (f32[320]{0:T(512)}, f32[320]{0:T(512)S(1)}, u32[]{:S(2)}) copy-start(f32[320]{0:T(512)S(1)} %broadcast_multiply_fusion.5) | copy-start | bytes 3844
  11.4 63.0 %copy-start.18 = (f32[320]{0:T(512)}, f32[320]{0:T(512)S(1)}, u32[]{:S(2)}) copy-start(f32[320]{0:T(512)S(1)} %add_rsqrt_fusion.1) | copy-start | bytes 3844
  78.0 3.0 copy-start.15
  78.0 3.7 copy-start.11
  78.0 4.4 copy-start.12
  79.1 140.3 %all-gather.20.cloned.1.call-start = ((), (), s32[]{:S(2)}) async-start(), calls=%async_computation.12 | async-start | bytes 4423680 | tf_op jit(solution)/shard_map/all_gather | solution.py:147
  79.8 259.0 %all-gather.10.cloned.1.call-start = ((), (), s32[]{:S(2)}) async-start(), calls=%async_computation.7 | async-start | bytes 8847360 | tf_op jit(solution)/shard_map/all_gather | solution.py:86
  80.9 326.7 %all-gather.12.cloned.1.call-start = ((), (), s32[]{:S(2)}) async-start(), calls=%async_computation.8 | async-start | bytes 1216512 | tf_op jit(solution)/shard_map/all_gather | solution.py:65
  81.6 378.8 %all-gather.14.cloned.1.call-start = ((), (), s32[]{:S(2)}) async-start(), calls=%async_computation.9 | async-start | bytes 4866048 | tf_op jit(solution)/shard_map/all_gather | solution.py:66
  82.4 444.1 %all-gather.16.cloned.1.call-start = ((), (), s32[]{:S(2)}) async-start(), calls=%async_computation.10 | async-start | bytes 4866048 | tf_op jit(solution)/shard_map/all_gather | solution.py:67
  83.1 584.7 %reduce-scatter.19.cloned.1.call-start = ((), (), s32[]{:S(2)}) async-start(), calls=%async_computation.17 | async-start | bytes 4423680
  84.1 442.3 %copy-start.21 = (f32[320]{0:T(512)}, f32[320]{0:T(512)S(1)}, u32[]{:S(2)}) copy-start(f32[320]{0:T(512)S(1)} %fusion.56) | copy-start | bytes 3844
  373.7 18.1 %copy-start.4 = (bf16[2560,768]{0,1:T(8,128)(2,1)S(1)}, bf16[2560,768]{0,1:T(8,128)(2,1)}, u32[]{:S(2)}) copy-start(bf16[2560,768]{0,1:T(8,128)(2,1)} %copy.34) | copy-start | bytes 11796484
  391.8 15.8 %copy-start = (bf16[320,768]{1,0:T(8,128)(2,1)S(1)}, bf16[320,768]{1,0:T(8,128)(2,1)}, u32[]{:S(2)}) copy-start(bf16[320,768]{1,0:T(8,128)(2,1)} %param.9) | copy-start | bytes 1474564
  407.6 58.8 %copy-start.1 = (bf16[320,12,64]{0,2,1:T(8,128)(2,1)}, bf16[320,12,64]{0,2,1:T(8,128)(2,1)S(1)}, u32[]{:S(2)}) copy-start(bf16[320,12,64]{0,2,1:T(8,128)(2,1)S(1)} %divide_convert_fusion) | copy-start | bytes 1474564
  407.6 52.9 %copy-start.13 = (f32[768]{0:T(1024)S(1)}, f32[768]{0:T(1024)}, u32[]{:S(2)}) copy-start(f32[768]{0:T(1024)} %param.17) | copy-start | bytes 9220
  410.7 115.8 %copy-start.9 = (bf16[320,768]{1,0:T(8,128)(2,1)S(1)}, bf16[320,768]{1,0:T(8,128)(2,1)}, u32[]{:S(2)}) copy-start(bf16[320,768]{1,0:T(8,128)(2,1)} %param.11) | copy-start | bytes 1474564
  526.5 7.4 copy-start.25
  533.8 2.5 copy-start.8
  533.8 2.5 copy-start.22
  533.9 2.9 copy-start.3
  584.5 1.1 copy-start.7
  584.5 1.1 copy-start.20
  584.6 171.5 %reduce-scatter.21.cloned.1.call-start = ((), (), s32[]{:S(2)}) async-start(), calls=%async_computation.18 | async-start | bytes 4423680
  610.2 1.1 copy-start.2
  610.3 3.3 copy-start.10
  610.3 3.3 copy-start.23
  610.3 250.3 %reduce-scatter.13.cloned.1.call-start = ((), (), s32[]{:S(2)}) async-start(), calls=%async_computation.14 | async-start | bytes 2433024 | tf_op jit(solution)/shard_map/reduce_scatter | solution.py:196
  613.5 389.1 %reduce-scatter.17.cloned.1.call-start = ((), (), s32[]{:S(2)}) async-start(), calls=%async_computation.16 | async-start | bytes 9732096 | tf_op jit(solution)/shard_map/reduce_scatter | solution.py:198
  622.3 521.3 %reduce-scatter.15.cloned.1.call-start = ((), (), s32[]{:S(2)}) async-start(), calls=%async_computation.15 | async-start | bytes 9732096 | tf_op jit(solution)/shard_map/reduce_scatter | solution.py:197
  629.3 128.9 %copy-start.14 = (f32[768]{0:T(1024)S(1)}, f32[768]{0:T(1024)}, u32[]{:S(2)}) copy-start(f32[768]{0:T(1024)} %param.16) | copy-start | bytes 9220
  629.3 128.9 %copy-start.17 = (f32[320]{0:T(512)S(1)}, f32[320]{0:T(512)}, u32[]{:S(2)}) copy-start(f32[320]{0:T(512)} %copy-done.16) | copy-start | bytes 3844
  629.3 128.8 %copy-start.19 = (f32[320]{0:T(512)S(1)}, f32[320]{0:T(512)}, u32[]{:S(2)}) copy-start(f32[320]{0:T(512)} %copy-done.18) | copy-start | bytes 3844
  629.3 639.5 %reduce-scatter.11.cloned.1.call-start = ((), (), s32[]{:S(2)}) async-start(), calls=%async_computation.13 | async-start | bytes 7299072 | tf_op jit(solution)/shard_map/reduce_scatter | solution.py:195
  764.6 6.9 copy-start.5
  764.6 6.9 copy-start.6
  764.6 6.9 copy-start.26
  771.5 1.9 copy-start.24
Sparse Core Ops, SparseCore 0:
  11.5 62.8 all-gather.7
  79.2 68.8 all-gather.17
  150.9 68.4 all-gather.19
  222.0 116.7 all-gather.9
  342.1 52.2 all-gather.11
  397.8 62.6 all-gather.13
  463.9 62.4 all-gather.15
  584.7 83.1 reduce-scatter.18
  672.0 84.0 reduce-scatter.20
  761.8 98.8 reduce-scatter.12
  868.1 134.5 reduce-scatter.16
  1009.0 134.5 reduce-scatter.14
  1150.8 117.9 reduce-scatter.10
